TPU v7x, 768 devices: a whole 4x8x12 slice. The times are simulated.
768 devices in a mesh: seq: 64 (over y, x, core), fsdp: 12 (over z).
Axes of the slice: x: 4, y: 8, z: 12, core: 2. Of those that a mesh axis runs over, the one named last changes fastest.
Arguments:
- features: bfloat16 [12, 8192, 4608], P('fsdp', 'seq'), may hold values from -6 to 6
- value_weight: bfloat16 [4608, 512], P(('seq', 'fsdp')), may hold values from -0.09375 to 0.09375
- queries: bfloat16 [12, 8192, 4096], P('fsdp', 'seq'), may hold values from -6 to 6
- key_states: bfloat16 [12, 8192, 512], P('fsdp', 'seq'), may hold values from -6 to 6
- out_grad: bfloat16 [12, 8192, 4096], P('fsdp', 'seq'), may hold values from -6 to 6
- doc_lengths: int32 [12, 64], P('fsdp'), may hold values from 1 to 256, 8192 in all within a row
Outputs:
- key_grad: bfloat16 [12, 8192, 512], P('fsdp', 'seq')
- feature_grad: bfloat16 [12, 8192, 4608], P('fsdp', 'seq')
Inputs may be any that keep to these rules, and one draw needn't show every extreme that they name: `doc_lengths`: each row sums to 8192; the longest document of each row has exactly 256 tokens.
All inputs are finite; a program needn't handle non-finite values.
Results may differ from a plain program's by a relative error of at most 0.008.
Values may be sent and summed in bfloat16 or wider, within the bound.
No kernel may reach another device: no remote copies, remote signals or barrier semaphores. Data moves between devices by JAX's collectives and lax.ppermute only.
A program may use at most 64 MiB of HBM per device.

v0:
```python
import math

import jax
import jax.numpy as jnp
from jax import lax
from jax.sharding import PartitionSpec as P

KVHEADS = 4
HEAD = 128
GROUP = 8


def from_behind(block, axis, distance):
    devices = range(lax.axis_size(axis))
    route = [(i - distance, i) for i in devices if i - distance in devices]
    return lax.ppermute(block, axis, route)


def doc_starts(doc_lens, positions):
    doc_ends = jnp.cumsum(doc_lens)
    taken = jnp.where(doc_ends[None, :] <= positions[:, None], doc_lens[None, :], 0)
    return jnp.sum(taken, axis=1)


def block_grads(query_block, key_window, value_window, grad_block, query_pos, key_pos, starts):
    score_scale = 1.0 / math.sqrt(HEAD)
    visible = (key_pos[None, :] >= starts[:, None]) & (key_pos[None, :] <= query_pos[:, None])
    count_rows = query_block.shape[0]
    key_parts = []
    value_parts = []
    for head_index in range(KVHEADS):
        lower = head_index * GROUP * HEAD
        upper = lower + GROUP * HEAD
        query_head = query_block[:, lower:upper].reshape(count_rows, GROUP, HEAD)
        grad_head = grad_block[:, lower:upper].reshape(count_rows, GROUP, HEAD)
        key_head = key_window[:, head_index * HEAD : (head_index + 1) * HEAD]
        value_head = value_window[:, head_index * HEAD : (head_index + 1) * HEAD]
        scores = (
            jnp.einsum("tgd,sd->gts", query_head, key_head, preferred_element_type=jnp.float32)
            * score_scale
        )
        scores = jnp.where(visible[None], scores, jnp.float32(-1e30))
        row_max = jnp.max(scores, axis=-1, keepdims=True)
        powers = jnp.exp(scores - row_max)
        probs = powers / jnp.sum(powers, axis=-1, keepdims=True)
        probs_low = probs.astype(jnp.bfloat16)
        attended = jnp.einsum(
            "gts,sd->tgd", probs_low, value_head, preferred_element_type=jnp.float32
        )
        delta = jnp.einsum("tgd,tgd->gt", grad_head.astype(jnp.float32), attended)
        dprob = jnp.einsum("tgd,sd->gts", grad_head, value_head, preferred_element_type=jnp.float32)
        dscore = (probs * (dprob - delta[:, :, None])).astype(jnp.bfloat16)
        key_part = (
            jnp.einsum("gts,tgd->sd", dscore, query_head, preferred_element_type=jnp.float32)
            * score_scale
        )
        value_part = jnp.einsum(
            "gts,tgd->sd", probs_low, grad_head, preferred_element_type=jnp.float32
        )
        key_parts.append(key_part)
        value_parts.append(value_part)
    return (jnp.concatenate(key_parts, axis=1), jnp.concatenate(value_parts, axis=1))


def previous(tensors, offset):
    return from_behind((tensors[0], tensors[1]), "seq", offset)


def returned(tensors, offset):
    return from_behind((tensors[0], tensors[1]), "seq", offset)


def shards(features, value_weight, queries, key_states, out_grad, doc_lengths):
    shard_rows = features.shape[1]
    feats = features[0]
    query_here = queries[0]
    key_here = key_states[0]
    grad_here = out_grad[0]
    doc_lens = doc_lengths[0]
    whole_weight = lax.all_gather(value_weight, ("seq", "fsdp"), axis=0, tiled=True)
    values = jnp.dot(feats, whole_weight, preferred_element_type=jnp.float32).astype(jnp.bfloat16)
    near_pair = previous((key_here, values), 1)
    far_pair = previous((key_here, values), 2)
    key_window = jnp.concatenate([far_pair[0], near_pair[0], key_here], axis=0)
    value_window = jnp.concatenate([far_pair[1], near_pair[1], values], axis=0)
    shard_index = lax.axis_index("seq")
    query_pos = shard_index * shard_rows + jnp.arange(shard_rows, dtype=jnp.int32)
    key_pos = (shard_index - 2) * shard_rows + jnp.arange(3 * shard_rows, dtype=jnp.int32)
    starts = doc_starts(doc_lens, query_pos)
    key_window_grad, value_window_grad = block_grads(
        query_here, key_window, value_window, grad_here, query_pos, key_pos, starts
    )
    far_slot = (key_window_grad[:shard_rows], value_window_grad[:shard_rows])
    near_slot = (
        key_window_grad[shard_rows : 2 * shard_rows],
        value_window_grad[shard_rows : 2 * shard_rows],
    )
    own_slot = (key_window_grad[2 * shard_rows :], value_window_grad[2 * shard_rows :])
    from_next = returned(near_slot, -1)
    from_far = returned(far_slot, -2)
    key_total = own_slot[0] + from_next[0] + from_far[0]
    value_total = own_slot[1] + from_next[1] + from_far[1]
    key_grad = key_total.astype(jnp.bfloat16)
    value_grad = value_total.astype(jnp.bfloat16)
    feature_grad = lax.dot_general(
        value_grad, whole_weight, (((1,), (1,)), ((), ())), preferred_element_type=jnp.float32
    ).astype(jnp.bfloat16)
    return (key_grad[None], feature_grad[None])


def solution(mesh):
    in_specs = (
        P("fsdp", "seq", None),
        P(("seq", "fsdp"), None),
        P("fsdp", "seq", None),
        P("fsdp", "seq", None),
        P("fsdp", "seq", None),
        P("fsdp", None),
    )
    out_specs = (P("fsdp", "seq", None), P("fsdp", "seq", None))
    return jax.shard_map(shards, mesh=mesh, in_specs=in_specs, out_specs=out_specs, check_vma=False)
```

profile of v0, /device:TPU:30, one launch (start us, length us, event | category | flops | bytes accessed | tf_op | source)
XLA Modules:
  0.0 256.1 jit_solution(660300274779009214)
XLA Ops:
  7.9 1.9 collective-permute-start.1
  9.8 4.6 %collective-permute-start = (bf16[128,512]{1,0:T(8,128)(2,1)}, bf16[128,512]{1,0:T(8,128)(2,1)}, u32[]{:S(2)}, u32[]{:S(2)}) collective-permute-start(bf16[128,512]{1,0:T(8,128)(2,1)} %bitcast.276), channel_id=1, source_target_pairs={{0,24},{12,36},{24,48},{36,60},{48,72},{60,84},{72,96},{84,108},{9... | collective-permute-start | bytes 393224 | tf_op jit(solution)/shard_map/ppermute | solution.py:16
  15.4 1.6 copy.101
  17.1 1.6 copy.103
  20.8 1.1 pad_maximum_fusion.2
  21.9 2.7 %fusion.76 = (f32[8,128]{1,0:T(8,128)S(1)}, f32[8,128,384]{1,2,0:T(8,128)}) fusion(bf16[128,8,128]{0,2,1:T(8,128)(2,1)} %bitcast.273, pred[128,384]{0,1:T(8,128)(4,1)S(1)} %compare_and_fusion, bf16[384,512]{1,0:T(8,128)(2,1)S(1)} %pad_maximum_fusion.2), kind=kOutput, calls=%fused_computation.112 | convolution fusion | flops 102236544 | bytes 1986560 | tf_op jit(solution)/shard_map/sub | solution.py:44
  24.6 1.6 fusion.53
  27.0 1.0 convolution_bitcast_fusion.4
  28.1 1.7 fusion.79
  29.8 1.6 fusion.50
  32.5 1.8 fusion.77
  34.3 1.5 fusion.52
  35.8 1.0 convolution_bitcast_fusion.5
  36.9 2.7 %fusion.78 = (f32[8,128]{1,0:T(8,128)S(1)}, f32[8,128,384]{1,2,0:T(8,128)}) fusion(bf16[128,8,128]{0,2,1:T(8,128)(2,1)} %bitcast.267, pred[128,384]{0,1:T(8,128)(4,1)S(1)} %copy-done.23, bf16[384,512]{1,0:T(8,128)(2,1)S(1)} %pad_maximum_fusion.2), kind=kOutput, calls=%fused_computation.114 | convolution fusion | flops 102236544 | bytes 1986560 | tf_op jit(solution)/shard_map/sub | solution.py:44
  39.6 1.6 fusion.51
  42.6 148.4 %all-gather.3.cloned.1.call-done = bf16[768,6,512]{2,1,0:T(8,128)(2,1)} async-done(((bf16[1,6,512]{2,1,0:T(8,128)(2,1)}), bf16[768,6,512]{2,1,0:T(8,128)(2,1)}) %all-gather.3.cloned.1.call-update) | async-done | bytes 4718608 | tf_op jit(solution)/shard_map/all_gather | solution.py:80
  191.0 8.8 %reshape.137 = bf16[4608,512]{1,0:T(8,128)(2,1)} reshape(bf16[768,6,512]{2,1,0:T(8,128)(2,1)} %all-gather.3.cloned.1.call-done) | data formatting | bytes 9437184
  199.8 3.2 %fusion.35 = bf16[128,512]{1,0:T(8,128)(2,1)S(1)} fusion(bf16[4608,512]{1,0:T(8,128)(2,1)} %reshape.137, bf16[1,128,4608]{2,1,0:T(8,128)(2,1)S(1)} %copy-done), kind=kOutput, calls=%fused_computation.52 | convolution fusion | flops 604045312 | bytes 6029312 | tf_op jit(solution)/shard_map/dot_general | solution.py:81
  203.0 2.3 collective-permute-start.3
  205.3 5.5 %collective-permute-start.2 = (bf16[128,512]{1,0:T(8,128)(2,1)S(1)}, bf16[128,512]{1,0:T(8,128)(2,1)S(1)}, u32[]{:S(2)}, u32[]{:S(2)}) collective-permute-start(bf16[128,512]{1,0:T(8,128)(2,1)S(1)} %fusion.35), channel_id=1, source_target_pairs={{0,24},{12,36},{24,48},{36,60},{48,72},{60,84},{72,96},{84,108},{9... | collective-permute-start | bytes 393224 | tf_op jit(solution)/shard_map/ppermute | solution.py:16
  211.7 3.1 %collective-permute-start.6 = (f32[128,512]{0,1:T(8,128)}, f32[128,512]{0,1:T(8,128)}, u32[]{:S(2)}, u32[]{:S(2)}) collective-permute-start(f32[128,512]{0,1:T(8,128)} %get-tuple-element.20), channel_id=1, source_target_pairs={{12,0},{24,12},{36,24},{48,36},{60,48},{72,60},{84,72},{96,84},{10... | collective-permute-start | bytes 786440 | tf_op jit(solution)/shard_map/ppermute | solution.py:16
  214.8 1.9 collective-permute-start.7
  218.5 2.8 %fusion.45 = f32[384,128]{0,1:T(8,128)} fusion(bf16[128,8,128]{0,2,1:T(8,128)(2,1)} %bitcast.274, bf16[128,8,128]{0,2,1:T(8,128)(2,1)} %bitcast.265, f32[8,128]{1,0:T(8,128)} %fusion.34, f32[8,128,384]{1,2,0:T(8,128)} %get-tuple-element.25, f32[8,128]{1,0:T(8,128)S(1)} %get-tuple-element.24, bf16[384,512]{1,0:T(8,128)(2,1)} %copy-done.11), kind=kOutput, calls=%fused_computation.60 | convolution fusion | flops 202948608 | bytes 2400256 | tf_op jit(solution)/shard_map/gts,tgd->sd/dot_general | solution.py:54
  221.2 1.3 fusion.31
  222.6 2.8 %fusion.42 = f32[384,128]{0,1:T(8,128)} fusion(bf16[128,8,128]{0,2,1:T(8,128)(2,1)} %bitcast.271, bf16[128,8,128]{0,2,1:T(8,128)(2,1)} %bitcast.263, f32[8,128]{1,0:T(8,128)S(1)} %fusion.31, f32[8,128,384]{1,2,0:T(8,128)} %get-tuple-element.31, f32[8,128]{1,0:T(8,128)S(1)} %get-tuple-element.30, bf16[384,512]{1,0:T(8,128)(2,1)} %copy-done.11), kind=kOutput, calls=%fused_computation.57 | convolution fusion | flops 202948608 | bytes 2400256 | tf_op jit(solution)/shard_map/gts,tgd->sd/dot_general | solution.py:54
  225.4 1.2 fusion.33
  226.7 2.1 fusion.44
  229.1 2.0 fusion.43
  231.3 1.9 collective-permute-start.4
  233.2 1.9 collective-permute-start.5
  235.2 5.3 %fusion.4 = bf16[1,128,4608]{2,1,0:T(8,128)(2,1)} fusion(bf16[4608,512]{1,0:T(8,128)(2,1)} %reshape.137, f32[128,512]{0,1:T(8,128)} %collective-permute-done.7, f32[128,512]{0,1:T(8,128)} %collective-permute-done.6, f32[384,512]{0,1:T(8,128)} %pad_maximum_fusion.1), kind=kOutput, calls=%fused_computation.5 | convolution fusion | flops 604766208 | bytes 6684672 | tf_op jit(solution)/shard_map/dot_general | solution.py:105
  240.4 8.0 %collective-permute-done.5 = f32[128,512]{0,1:T(8,128)S(1)} collective-permute-done((f32[128,512]{0,1:T(8,128)S(1)}, f32[128,512]{0,1:T(8,128)S(1)}, u32[]{:S(2)}, u32[]{:S(2)}) %collective-permute-start.5) | collective-permute-done | bytes 262176 | tf_op jit(solution)/shard_map/ppermute | solution.py:16
  (79 shorter events, 10.8 us)
Async XLA Ops:
  7.2 192.6 %copy-start = (bf16[1,128,4608]{2,1,0:T(8,128)(2,1)S(1)}, bf16[1,128,4608]{2,1,0:T(8,128)(2,1)}, u32[]{:S(2)}) copy-start(bf16[1,128,4608]{2,1,0:T(8,128)(2,1)} %param.6) | copy-start | bytes 3538948
  7.2 183.8 %all-gather.3.cloned.1.call-start = ((), (), s32[]{:S(2)}) async-start(), calls=%async_computation | async-start | bytes 6299648 | tf_op jit(solution)/shard_map/all_gather | solution.py:80
  7.9 12.9 %collective-permute-start.1 = (bf16[128,512]{1,0:T(8,128)(2,1)}, bf16[128,512]{1,0:T(8,128)(2,1)S(1)}, u32[]{:S(2)}, u32[]{:S(2)}) collective-permute-start(bf16[128,512]{1,0:T(8,128)(2,1)} %bitcast.275), channel_id=1, source_target_pairs={{0,12},{12,24},{24,36},{36,48},{48,60},{60,72},{72,84},{84,96},{96... | collective-permute-start | bytes 393224 | tf_op jit(solution)/shard_map/ppermute | solution.py:16
  9.8 10.9 %collective-permute-start = (bf16[128,512]{1,0:T(8,128)(2,1)}, bf16[128,512]{1,0:T(8,128)(2,1)}, u32[]{:S(2)}, u32[]{:S(2)}) collective-permute-start(bf16[128,512]{1,0:T(8,128)(2,1)} %bitcast.276), channel_id=1, source_target_pairs={{0,24},{12,36},{24,48},{36,60},{48,72},{60,84},{72,96},{84,108},{9... | collective-permute-start | bytes 393224 | tf_op jit(solution)/shard_map/ppermute | solution.py:16
  17.1 1.7 copy-start.24
  19.9 0.9 copy-start.21
  20.6 9.2 %copy-start.9 = (bf16[128,1024]{0,1:T(8,128)(2,1)}, bf16[128,1024]{0,1:T(8,128)(2,1)S(1)}, u32[]{:S(2)}) copy-start(bf16[128,1024]{0,1:T(8,128)(2,1)S(1)} %get-tuple-element.13) | copy-start | bytes 786436
  20.6 10.8 %copy-start.8 = (bf16[128,1024]{0,1:T(8,128)(2,1)}, bf16[128,1024]{0,1:T(8,128)(2,1)S(1)}, u32[]{:S(2)}) copy-start(bf16[128,1024]{0,1:T(8,128)(2,1)S(1)} %get-tuple-element.12) | copy-start | bytes 786436
  20.6 15.2 %copy-start.6 = (bf16[128,1024]{0,1:T(8,128)(2,1)}, bf16[128,1024]{0,1:T(8,128)(2,1)S(1)}, u32[]{:S(2)}) copy-start(bf16[128,1024]{0,1:T(8,128)(2,1)S(1)} %get-tuple-element.14) | copy-start | bytes 786436
  20.8 7.3 %copy-start.22 = (pred[128,384]{0,1:T(8,128)(4,1)}, pred[128,384]{0,1:T(8,128)(4,1)S(1)}, u32[]{:S(2)}) copy-start(pred[128,384]{0,1:T(8,128)(4,1)S(1)} %compare_and_fusion) | copy-start | bytes 147460
  24.6 3.5 %copy-start.18 = (bf16[128,1024]{0,1:T(8,128)(2,1)S(1)}, bf16[128,1024]{0,1:T(8,128)(2,1)}, u32[]{:S(2)}) copy-start(bf16[128,1024]{0,1:T(8,128)(2,1)} %get-tuple-element.16) | copy-start | bytes 786436
  29.8 2.6 %copy-start.17 = (bf16[128,1024]{0,1:T(8,128)(2,1)S(1)}, bf16[128,1024]{0,1:T(8,128)(2,1)}, u32[]{:S(2)}) copy-start(bf16[128,1024]{0,1:T(8,128)(2,1)} %get-tuple-element.18) | copy-start | bytes 786436
  29.8 2.6 %copy-start.23 = (pred[128,384]{0,1:T(8,128)(4,1)S(1)}, pred[128,384]{0,1:T(8,128)(4,1)}, u32[]{:S(2)}) copy-start(pred[128,384]{0,1:T(8,128)(4,1)} %copy-done.22) | copy-start | bytes 147460
  39.6 1.6 copy-start.4
  39.6 2.0 copy-start.13
  39.6 2.0 copy-start.14
  39.6 2.0 copy-start.15
  199.8 11.0 %copy-start.3 = (f32[384,512]{0,1:T(8,128)S(1)}, f32[384,512]{0,1:T(8,128)}, u32[]{:S(2)}) copy-start(f32[384,512]{0,1:T(8,128)} %pad_maximum_fusion.1) | copy-start | bytes 2359300
  203.0 14.5 %copy-start.2 = (bf16[8,128,384]{1,2,0:T(8,128)(2,1)S(1)}, bf16[8,128,384]{1,2,0:T(8,128)(2,1)}, u32[]{:S(2)}) copy-start(bf16[8,128,384]{1,2,0:T(8,128)(2,1)} %copy-done.1) | copy-start | bytes 2359300
  203.0 14.5 %copy-start.10 = (bf16[128,1024]{0,1:T(8,128)(2,1)S(1)}, bf16[128,1024]{0,1:T(8,128)(2,1)}, u32[]{:S(2)}) copy-start(bf16[128,1024]{0,1:T(8,128)(2,1)} %copy-done.9) | copy-start | bytes 786436
  203.0 13.7 %collective-permute-start.3 = (bf16[128,512]{1,0:T(8,128)(2,1)S(1)}, bf16[128,512]{1,0:T(8,128)(2,1)S(1)}, u32[]{:S(2)}, u32[]{:S(2)}) collective-permute-start(bf16[128,512]{1,0:T(8,128)(2,1)S(1)} %fusion.35), channel_id=1, source_target_pairs={{0,12},{12,24},{24,36},{36,48},{48,60},{60,72},{72,84},{84,96},{96... | collective-permute-start | bytes 393224 | tf_op jit(solution)/shard_map/ppermute | solution.py:16
  205.3 11.4 %collective-permute-start.2 = (bf16[128,512]{1,0:T(8,128)(2,1)S(1)}, bf16[128,512]{1,0:T(8,128)(2,1)S(1)}, u32[]{:S(2)}, u32[]{:S(2)}) collective-permute-start(bf16[128,512]{1,0:T(8,128)(2,1)S(1)} %fusion.35), channel_id=1, source_target_pairs={{0,24},{12,36},{24,48},{36,60},{48,72},{60,84},{72,96},{84,108},{9... | collective-permute-start | bytes 393224 | tf_op jit(solution)/shard_map/ppermute | solution.py:16
  211.7 23.5 %collective-permute-start.6 = (f32[128,512]{0,1:T(8,128)}, f32[128,512]{0,1:T(8,128)}, u32[]{:S(2)}, u32[]{:S(2)}) collective-permute-start(f32[128,512]{0,1:T(8,128)} %get-tuple-element.20), channel_id=1, source_target_pairs={{12,0},{24,12},{36,24},{48,36},{60,48},{72,60},{84,72},{96,84},{10... | collective-permute-start | bytes 786440 | tf_op jit(solution)/shard_map/ppermute | solution.py:16
  214.8 20.3 %collective-permute-start.7 = (f32[128,512]{0,1:T(8,128)}, f32[128,512]{0,1:T(8,128)}, u32[]{:S(2)}, u32[]{:S(2)}) collective-permute-start(f32[128,512]{0,1:T(8,128)} %get-tuple-element.21), channel_id=1, source_target_pairs={{24,0},{36,12},{48,24},{60,36},{72,48},{84,60},{96,72},{108,84},{1... | collective-permute-start | bytes 786440 | tf_op jit(solution)/shard_map/ppermute | solution.py:16
  222.6 2.8 %copy-start.7 = (bf16[128,1024]{0,1:T(8,128)(2,1)S(1)}, bf16[128,1024]{0,1:T(8,128)(2,1)}, u32[]{:S(2)}) copy-start(bf16[128,1024]{0,1:T(8,128)(2,1)} %copy-done.6) | copy-start | bytes 786436
  226.6 2.1 copy-start.5
  226.6 2.1 copy-start.12
  226.7 2.5 copy-start.16
  229.1 2.0 copy-start.19
  229.1 2.0 copy-start.20
  231.3 9.2 %collective-permute-start.4 = (f32[128,512]{0,1:T(8,128)S(1)}, f32[128,512]{0,1:T(8,128)S(1)}, u32[]{:S(2)}, u32[]{:S(2)}) collective-permute-start(f32[128,512]{0,1:T(8,128)S(1)} %get-tuple-element.22), channel_id=1, source_target_pairs={{12,0},{24,12},{36,24},{48,36},{60,48},{72,60},{84,72},{96,84},{10... | collective-permute-start | bytes 786440 | tf_op jit(solution)/shard_map/ppermute | solution.py:16
  233.2 15.3 %collective-permute-start.5 = (f32[128,512]{0,1:T(8,128)S(1)}, f32[128,512]{0,1:T(8,128)S(1)}, u32[]{:S(2)}, u32[]{:S(2)}) collective-permute-start(f32[128,512]{0,1:T(8,128)S(1)} %get-tuple-element.23), channel_id=1, source_target_pairs={{24,0},{36,12},{48,24},{60,36},{72,48},{84,60},{96,72},{108,84},{1... | collective-permute-start | bytes 786440 | tf_op jit(solution)/shard_map/ppermute | solution.py:16
  (2 other events, 1.6 us)
Sparse Core Ops, SparseCore 0:
  13.5 177.3 all-gather.2
where the time goes:
time: 257 us; the launch traced here: 256 us
  waiting for transfers between devices  157 us (61%)
  matrix products  34.4 us (13%)
  starting transfers between devices  23.3 us (9%)
  local copies, waits for them, and re-layouts  17.9 us (7%)
  between operations  14.5 us (6%)
  other arithmetic  8.89 us (3%)
    all_gather x1, waiting for transfers between devices, shards(): lax.all_gather(value_weight, ('seq', 'fsdp'), axis=0, tiled=True)  148 us
    ppermute x8, starting transfers between devices, from_behind(): return lax.ppermute(block, axis, route)  23.2 us
    unnamed x54, local copies, waits for them, and re-layouts  14.5 us
    dot_general x4, matrix products, block_grads(): jnp.einsum('gts,tgd->sd', dscore, query_head, preferred_element_type=jnp....  9.67 us
    sub x4, matrix products, block_grads(): powers = jnp.exp(scores - row_max)  8.92 us
    ppermute x8, waiting for transfers between devices, from_behind(): return lax.ppermute(block, axis, route)  8.05 us
    convert_element_type x4, other arithmetic, block_grads(): probs_low = probs.astype(jnp.bfloat16)  6.33 us
    dot_general x1, matrix products, shards(): lax.dot_general(value_grad, whole_weight, (((1,), (1,)), ((), ())), prefe...  5.29 us
  transfers between devices with their start and end apart: 9, of which 2 were waited for; matrix products, arithmetic and copies ran while one was open for 18% of the time, Pallas kernels for 0%

commit v1 on v0

v1 whole, which is shorter than its diff:
```python
import math

import jax
import jax.numpy as jnp
from jax import lax
from jax.experimental import pallas as pl
from jax.experimental.pallas import tpu as pltpu
from jax.sharding import Mesh, PartitionSpec as P

KVHEADS = 4
HEAD = 128
GROUP = 8
PAIR = 2
NEG = -1e30
VMEM_LIMIT = 12 << 20
COST = pl.CostEstimate(flops=2 * 10**9, bytes_accessed=9 * 10**6, transcendentals=2 * 10**6)


def stacked(ref, first, count):
    return jnp.concatenate(
        [ref[:, (first + i) * HEAD : (first + i + 1) * HEAD] for i in range(count)], axis=0
    )


def probs_kernel(start_ref, q_ref, g_ref, kf_ref, kn_ref, ko_ref, p_ref, vf_ref, vn_ref, vo_ref, low_ref):
    rows = q_ref.shape[0]
    keys = jnp.concatenate([kf_ref[...], kn_ref[...], ko_ref[...]], axis=0)
    shape = (3 * rows, PAIR * rows)
    key_pos = lax.broadcasted_iota(jnp.int32, shape, 0) - 2 * rows
    query_pos = lax.broadcasted_iota(jnp.int32, shape, 1) % rows
    starts = jnp.concatenate([start_ref[...]] * PAIR, axis=1)
    visible = (key_pos >= starts) & (key_pos <= query_pos)
    for pair in range(GROUP // PAIR):
        cols = slice(pair * PAIR * rows, (pair + 1) * PAIR * rows)
        query = stacked(q_ref, pair * PAIR, PAIR)
        scores = lax.dot_general(
            keys, query, (((1,), (1,)), ((), ())), preferred_element_type=jnp.float32
        ) * (1.0 / math.sqrt(HEAD))
        scores = jnp.where(visible, scores, NEG)
        powers = jnp.exp(scores - jnp.max(scores, axis=0, keepdims=True))
        probs = powers * (1.0 / jnp.sum(powers, axis=0, keepdims=True))
        p_ref[:, cols] = probs
        low_ref[:, cols] = probs.astype(jnp.bfloat16)
    part = lax.dot_general(
        low_ref[...], stacked(g_ref, 0, GROUP), (((1,), (0,)), ((), ())),
        preferred_element_type=jnp.float32,
    )
    vf_ref[...] = part[:rows].astype(vf_ref.dtype)
    vn_ref[...] = part[rows : 2 * rows].astype(vn_ref.dtype)
    vo_ref[...] = part[2 * rows :]


def grads_kernel(p_ref, q_ref, g_ref, vf_ref, vn_ref, vo_ref, kf_ref, kn_ref, ko_ref, ds_ref):
    rows = q_ref.shape[0]
    values = jnp.concatenate([vf_ref[...], vn_ref[...], vo_ref[...]], axis=0)
    for pair in range(GROUP // PAIR):
        cols = slice(pair * PAIR * rows, (pair + 1) * PAIR * rows)
        grad = stacked(g_ref, pair * PAIR, PAIR)
        dprob = lax.dot_general(
            values, grad, (((1,), (1,)), ((), ())), preferred_element_type=jnp.float32
        )
        probs = p_ref[:, cols]
        low = probs.astype(jnp.bfloat16).astype(jnp.float32)
        delta = jnp.sum(low * dprob, axis=0, keepdims=True)
        ds_ref[:, cols] = (probs * (dprob - delta)).astype(jnp.bfloat16)
    part = lax.dot_general(
        ds_ref[...], stacked(q_ref, 0, GROUP), (((1,), (0,)), ((), ())),
        preferred_element_type=jnp.float32,
    ) * (1.0 / math.sqrt(HEAD))
    kf_ref[...] = part[:rows].astype(kf_ref.dtype)
    kn_ref[...] = part[rows : 2 * rows].astype(kn_ref.dtype)
    ko_ref[...] = part[2 * rows :]


def specs(rows):
    wide = pl.BlockSpec((rows, GROUP * HEAD), lambda h: (0, h))
    head = pl.BlockSpec((rows, HEAD), lambda h: (0, h))
    probs = pl.BlockSpec((None, 3 * rows, GROUP * rows), lambda h: (h, 0, 0))
    shapes = [
        jax.ShapeDtypeStruct((rows, KVHEADS * HEAD), d) for d in (jnp.bfloat16, jnp.bfloat16, jnp.float32)
    ]
    return wide, head, probs, shapes


def probs_call(starts, query, grad, far, near, own):
    rows = query.shape[0]
    wide, head, probs, shapes = specs(rows)
    return pl.pallas_call(
        probs_kernel,
        grid=(KVHEADS,),
        in_specs=[pl.BlockSpec((1, rows), lambda h: (0, 0)), wide, wide, head, head, head],
        out_specs=[probs, head, head, head],
        out_shape=[pltpu.HBM((KVHEADS, 3 * rows, GROUP * rows), jnp.float32)] + shapes,
        scratch_shapes=[pltpu.VMEM((3 * rows, GROUP * rows), jnp.bfloat16)],
        compiler_params=pltpu.CompilerParams(vmem_limit_bytes=VMEM_LIMIT),
        cost_estimate=COST,
        name="probs",
    )(starts, query, grad, far, near, own)


def grads_call(probs_all, query, grad, far, near, own):
    rows = query.shape[0]
    wide, head, probs, shapes = specs(rows)
    return pl.pallas_call(
        grads_kernel,
        grid=(KVHEADS,),
        in_specs=[probs, wide, wide, head, head, head],
        out_specs=[head, head, head],
        out_shape=shapes,
        scratch_shapes=[pltpu.VMEM((3 * rows, GROUP * rows), jnp.bfloat16)],
        compiler_params=pltpu.CompilerParams(vmem_limit_bytes=VMEM_LIMIT),
        cost_estimate=COST,
        name="grads",
    )(probs_all, query, grad, far, near, own)


def from_behind(block, distance):
    axes = SEQ
    count = math.prod(lax.axis_size(a) for a in axes)
    route = [(i - distance, i) for i in range(count) if 0 <= i - distance < count]
    return lax.ppermute(block, axes, route)


def ring(block, axes, distance):
    count = math.prod(lax.axis_size(a) for a in axes)
    return lax.ppermute(block, axes, [(i, (i + distance) % count) for i in range(count)])


def doc_starts(doc_lens, positions):
    doc_ends = jnp.cumsum(doc_lens)
    taken = jnp.where(doc_ends[None, :] <= positions[:, None], doc_lens[None, :], 0)
    return jnp.sum(taken, axis=1)


def copies(block, axis):
    count = lax.axis_size(axis)
    return lax.all_to_all(jnp.broadcast_to(block[None], (count,) + block.shape), axis, 0, 0, tiled=True)


def gathered(weight):
    rows, width = weight.shape
    ny, nx, nc, nz = (lax.axis_size(a) for a in ("y", "x", "core", "z"))
    me, core, low = lax.axis_index("x"), lax.axis_index("core"), lax.axis_size("y") // 2
    mine = copies(weight, "z")
    mine = mine.reshape(nz * rows, width)
    mine = copies(mine, "y")
    first, second = mine[:low], mine[low:]
    left_a = ring(first, ("x",), 1)
    right_b = ring(second, ("x",), -1)
    left_b = ring(second, ("x",), 1)
    right_a = ring(first, ("x",), -1)
    far_a = ring(left_a, ("x",), 1)
    far_b = ring(right_b, ("x",), -1)
    early, late = (first, second, left_a, left_b, right_a, right_b), (far_a, far_b)
    early_swapped = ring(jnp.stack(early), ("core",), 1).reshape((3,) + mine.shape)
    late_swapped = ring(jnp.stack(late), ("core",), 1).reshape((1,) + mine.shape)
    slots = [((me + i) & (nx - 1)) * nc for i in (0, nx - 1, 1, 2)]
    whole = jnp.zeros((ny, nx * nc, nz * rows, width), weight.dtype)
    for i, piece in enumerate(early + late):
        whole = lax.dynamic_update_slice(whole, piece[:, None], (low * (i % 2), slots[i // 2] + core, 0, 0))
    for i, piece in enumerate([early_swapped[j] for j in range(3)] + [late_swapped[0]]):
        whole = lax.dynamic_update_slice(whole, piece[:, None], (0, slots[i] + 1 - core, 0, 0))
    return whole.reshape(ny * nx * nc * nz * rows, width)


def program(features, value_weight, queries, key_states, out_grad, doc_lengths):
    rows = features.shape[1]
    first = lax.axis_index(SEQ) * rows
    starts = doc_starts(doc_lengths[0], first + jnp.arange(rows, dtype=jnp.int32)) - first
    whole_weight = gathered(value_weight)
    keys = key_states[0]
    query, grad = (pltpu.with_memory_space_constraint(a[0], pltpu.HBM) for a in (queries, out_grad))
    keys_far = from_behind(keys, 2)
    keys_near = from_behind(keys, 1)
    probs, value_far, value_near, value_own = probs_call(
        starts[None], query, grad, keys_far, keys_near, keys
    )
    value_near = from_behind(value_near, -1)
    value_far = from_behind(value_far, -2)
    value_grad = (value_own + value_near + value_far).astype(jnp.bfloat16)
    values = jnp.dot(features[0], whole_weight, preferred_element_type=jnp.float32).astype(jnp.bfloat16)
    far = from_behind(values, 2)
    near = from_behind(values, 1)
    key_far, key_near, key_own = grads_call(probs, query, grad, far, near, values)
    feature_grad = lax.dot_general(
        value_grad, whole_weight, (((1,), (1,)), ((), ())), preferred_element_type=jnp.float32
    ).astype(jnp.bfloat16)
    key_far = from_behind(key_far, -2)
    key_near = from_behind(key_near, -1)
    key_grad = (key_own + key_near + key_far).astype(jnp.bfloat16)
    return (key_grad[None], feature_grad[None])


SEQ = ("y", "x", "core")


def solution(mesh):
    chips = Mesh(mesh.devices.reshape(8, 4, 2, 12), SEQ + ("z",))
    tokens = P("z", SEQ, None)
    in_specs = (tokens, P(SEQ + ("z",), None), tokens, tokens, tokens, P("z", None))
    return jax.shard_map(program, mesh=chips, in_specs=in_specs, out_specs=(tokens, tokens), check_vma=False)
```

time: 257 us -> 136 us (0.53)
  the two profiles are of different devices: /device:TPU:30 before, /device:TPU:6 now
where the time goes in v1:
time: 136 us; the launch traced here: 135 us
  starting transfers between devices  49.2 us (36%)
  waiting for transfers between devices  35.1 us (26%)
  blocking collectives  26.9 us (20%)
  Pallas kernels  11.6 us (9%)
  local copies, waits for them, and re-layouts  6.38 us (5%)
  matrix products  3.44 us (3%)
  other arithmetic  1.72 us (1%)
    all_to_all x1, blocking collectives, copies(): lax.all_to_all(jnp.broadcast_to(block[None], (count,) + block.shape), axi...  26.9 us
    ppermute x8, starting transfers between devices, from_behind(): return lax.ppermute(block, axes, route)  21.5 us
    ppermute x8, starting transfers between devices, ring(): lax.ppermute(block, axes, [(i, (i + distance) % count) for i in range(cou...  20.6 us
    ppermute x8, waiting for transfers between devices, ring(): lax.ppermute(block, axes, [(i, (i + distance) % count) for i in range(cou...  19.3 us
    all_to_all x1, waiting for transfers between devices, copies(): lax.all_to_all(jnp.broadcast_to(block[None], (count,) + block.shape), axi...  10.9 us
    all_to_all x1, starting transfers between devices, copies(): lax.all_to_all(jnp.broadcast_to(block[None], (count,) + block.shape), axi...  7.1 us
    pallas_call x1, Pallas kernels, probs_call(): pl.pallas_call(probs_kernel, grid=(KVHEADS,), in_specs=[pl.BlockSpec((1,...  6.69 us
    pallas_call x1, Pallas kernels, grads_call(): pl.pallas_call(grads_kernel, grid=(KVHEADS,), in_specs=[probs, wide, wide...  4.95 us
  transfers between devices with their start and end apart: 17, of which 8 were waited for; matrix products, arithmetic and copies ran while one was open for 5% of the time, Pallas kernels for 9%

profile of v1, /device:TPU:6, one launch (start us, length us, event | category | flops | bytes accessed | tf_op | source)
XLA Modules:
  0.0 135.4 jit_solution(12424511190961102497)
XLA Ops:
  0.6 0.8 broadcast_in_dim.67
  1.4 26.9 %all_to_all.10 = bf16[12,6,512]{2,1,0:T(8,128)(2,1)S(1)} all-to-all(bf16[12,6,512]{2,1,0:T(8,128)(2,1)S(1)} %broadcast_in_dim.67), channel_id=1, replica_groups=mesh['y'=8,'x'=4,'core'=2,'z'=12] {'z'}, dimensions={0} | all-to-all | bytes 147456 | tf_op jit(solution)/shard_map/all_to_all | solution.py:137
  28.4 0.9 broadcast_in_dim.69
  29.2 7.1 %all-to-all-start.1 = ((bf16[8,72,512]{2,1,0:T(8,128)(2,1)}), bf16[8,72,512]{2,1,0:T(8,128)(2,1)S(1)}, u32[]{:S(2)}, u32[]{:S(2)}) async-start(bf16[8,72,512]{2,1,0:T(8,128)(2,1)} %broadcast_in_dim.69), calls=%async_computation.1 | async-start | bytes 1179648 | tf_op jit(solution)/shard_map/all_to_all | solution.py:137
  36.3 3.8 %collective-permute-start = (bf16[128,512]{1,0:T(8,128)(2,1)}, bf16[128,512]{1,0:T(8,128)(2,1)S(1)}, u32[]{:S(2)}, u32[]{:S(2)}) collective-permute-start(bf16[128,512]{1,0:T(8,128)(2,1)} %bitcast.71), channel_id=1, source_target_pairs={{0,24},{12,36},{24,48},{36,60},{48,72},{60,84},{72,96},{84,108},{9... | collective-permute-start | bytes 393224 | tf_op jit(solution)/shard_map/ppermute | solution.py:121
  40.2 1.9 %collective-permute-start.1 = (bf16[128,512]{1,0:T(8,128)(2,1)}, bf16[128,512]{1,0:T(8,128)(2,1)S(1)}, u32[]{:S(2)}, u32[]{:S(2)}) collective-permute-start(bf16[128,512]{1,0:T(8,128)(2,1)} %bitcast.72), channel_id=1, source_target_pairs={{0,12},{12,24},{24,36},{36,48},{48,60},{60,72},{72,84},{84,96},{96... | collective-permute-start | bytes 393224 | tf_op jit(solution)/shard_map/ppermute | solution.py:121
  43.9 10.9 %all-to-all-done.1 = bf16[8,72,512]{2,1,0:T(8,128)(2,1)S(1)} async-done(((bf16[8,72,512]{2,1,0:T(8,128)(2,1)}), bf16[8,72,512]{2,1,0:T(8,128)(2,1)S(1)}, u32[]{:S(2)}, u32[]{:S(2)}) %all-to-all-start.1) | async-done | bytes 589856 | tf_op jit(solution)/shard_map/all_to_all | solution.py:137
  54.9 1.9 %collective-permute-start.2 = (bf16[4,72,512]{2,1,0:T(8,128)(2,1)S(1)}, bf16[4,72,512]{2,1,0:T(8,128)(2,1)S(1)}, u32[]{:S(2)}, u32[]{:S(2)}) collective-permute-start(bf16[4,72,512]{2,1,0:T(8,128)(2,1)S(1)} %get-tuple-element.20), channel_id=1, source_target_pairs={{0,24},{24,48},{48,72},{72,0},{1,25},{25,49},{49,73},{73,1},{2,26}... | collective-permute-start | bytes 884744 | tf_op jit(solution)/shard_map/ppermute | solution.py:126
  56.8 3.9 %collective-permute-start.4 = (bf16[4,72,512]{2,1,0:T(8,128)(2,1)S(1)}, bf16[4,72,512]{2,1,0:T(8,128)(2,1)S(1)}, u32[]{:S(2)}, u32[]{:S(2)}) collective-permute-start(bf16[4,72,512]{2,1,0:T(8,128)(2,1)S(1)} %get-tuple-element.20), channel_id=1, source_target_pairs={{0,72},{24,0},{48,24},{72,48},{1,73},{25,1},{49,25},{73,49},{2,74}... | collective-permute-start | bytes 884744 | tf_op jit(solution)/shard_map/ppermute | solution.py:126
  60.7 3.1 %collective-permute-start.3 = (bf16[4,72,512]{2,1,0:T(8,128)(2,1)S(1)}, bf16[4,72,512]{2,1,0:T(8,128)(2,1)S(1)}, u32[]{:S(2)}, u32[]{:S(2)}) collective-permute-start(bf16[4,72,512]{2,1,0:T(8,128)(2,1)S(1)} %get-tuple-element.19), channel_id=1, source_target_pairs={{0,24},{24,48},{48,72},{72,0},{1,25},{25,49},{49,73},{73,1},{2,26}... | collective-permute-start | bytes 884744 | tf_op jit(solution)/shard_map/ppermute | solution.py:126
  64.4 1.5 %collective-permute-done.2 = bf16[4,72,512]{2,1,0:T(8,128)(2,1)S(1)} collective-permute-done((bf16[4,72,512]{2,1,0:T(8,128)(2,1)S(1)}, bf16[4,72,512]{2,1,0:T(8,128)(2,1)S(1)}, u32[]{:S(2)}, u32[]{:S(2)}) %collective-permute-start.2) | collective-permute-done | bytes 294944 | tf_op jit(solution)/shard_map/ppermute | solution.py:126
  65.9 1.9 %collective-permute-start.5 = (bf16[4,72,512]{2,1,0:T(8,128)(2,1)S(1)}, bf16[4,72,512]{2,1,0:T(8,128)(2,1)S(1)}, u32[]{:S(2)}, u32[]{:S(2)}) collective-permute-start(bf16[4,72,512]{2,1,0:T(8,128)(2,1)S(1)} %get-tuple-element.19), channel_id=1, source_target_pairs={{0,72},{24,0},{48,24},{72,48},{1,73},{25,1},{49,25},{73,49},{2,74}... | collective-permute-start | bytes 884744 | tf_op jit(solution)/shard_map/ppermute | solution.py:126
  67.9 1.5 %collective-permute-done.3 = bf16[4,72,512]{2,1,0:T(8,128)(2,1)S(1)} collective-permute-done((bf16[4,72,512]{2,1,0:T(8,128)(2,1)S(1)}, bf16[4,72,512]{2,1,0:T(8,128)(2,1)S(1)}, u32[]{:S(2)}, u32[]{:S(2)}) %collective-permute-start.3) | collective-permute-done | bytes 294944 | tf_op jit(solution)/shard_map/ppermute | solution.py:126
  69.4 6.3 %collective-permute-done.5 = bf16[4,72,512]{2,1,0:T(8,128)(2,1)S(1)} collective-permute-done((bf16[4,72,512]{2,1,0:T(8,128)(2,1)S(1)}, bf16[4,72,512]{2,1,0:T(8,128)(2,1)S(1)}, u32[]{:S(2)}, u32[]{:S(2)}) %collective-permute-start.5) | collective-permute-done | bytes 294944 | tf_op jit(solution)/shard_map/ppermute | solution.py:126
  75.8 1.9 %collective-permute-start.8 = (bf16[6,4,72,512]{3,2,1,0:T(8,128)(2,1)S(1)}, bf16[6,4,72,512]{3,2,1,0:T(8,128)(2,1)S(1)}, u32[]{:S(2)}, u32[]{:S(2)}) collective-permute-start(bf16[6,4,72,512]{3,2,1,0:T(8,128)(2,1)S(1)} %bitcast_dynamic-update-slice_fusion.7), channel_id=1, source_target_pairs={{0,12},{12,0},{1,13},{13,1},{2,14},{14,2},{3,15},{15,3},{4,16},{16... | collective-permute-start | bytes 5308424 | tf_op jit(solution)/shard_map/ppermute | solution.py:126
  77.7 1.9 %collective-permute-start.6 = (bf16[4,72,512]{2,1,0:T(8,128)(2,1)S(1)}, bf16[4,72,512]{2,1,0:T(8,128)(2,1)S(1)}, u32[]{:S(2)}, u32[]{:S(2)}) collective-permute-start(bf16[4,72,512]{2,1,0:T(8,128)(2,1)S(1)} %collective-permute-done.2), channel_id=1, source_target_pairs={{0,24},{24,48},{48,72},{72,0},{1,25},{25,49},{49,73},{73,1},{2,26}... | collective-permute-start | bytes 884744 | tf_op jit(solution)/shard_map/ppermute | solution.py:126
  79.6 3.9 %collective-permute-start.7 = (bf16[4,72,512]{2,1,0:T(8,128)(2,1)S(1)}, bf16[4,72,512]{2,1,0:T(8,128)(2,1)S(1)}, u32[]{:S(2)}, u32[]{:S(2)}) collective-permute-start(bf16[4,72,512]{2,1,0:T(8,128)(2,1)S(1)} %collective-permute-done.5), channel_id=1, source_target_pairs={{0,72},{24,0},{48,24},{72,48},{1,73},{25,1},{49,25},{73,49},{2,74}... | collective-permute-start | bytes 884744 | tf_op jit(solution)/shard_map/ppermute | solution.py:126
  83.7 5.3 %collective-permute-done.6 = bf16[4,72,512]{2,1,0:T(8,128)(2,1)S(1)} collective-permute-done((bf16[4,72,512]{2,1,0:T(8,128)(2,1)S(1)}, bf16[4,72,512]{2,1,0:T(8,128)(2,1)S(1)}, u32[]{:S(2)}, u32[]{:S(2)}) %collective-permute-start.6) | collective-permute-done | bytes 294944 | tf_op jit(solution)/shard_map/ppermute | solution.py:126
  89.0 3.1 %collective-permute-done.7 = bf16[4,72,512]{2,1,0:T(8,128)(2,1)S(1)} collective-permute-done((bf16[4,72,512]{2,1,0:T(8,128)(2,1)S(1)}, bf16[4,72,512]{2,1,0:T(8,128)(2,1)S(1)}, u32[]{:S(2)}, u32[]{:S(2)}) %collective-permute-start.7) | collective-permute-done | bytes 294944 | tf_op jit(solution)/shard_map/ppermute | solution.py:126
  92.2 1.9 %collective-permute-start.9 = (bf16[2,4,72,512]{3,2,1,0:T(8,128)(2,1)S(1)}, bf16[2,4,72,512]{3,2,1,0:T(8,128)(2,1)S(1)}, u32[]{:S(2)}, u32[]{:S(2)}) collective-permute-start(bf16[2,4,72,512]{3,2,1,0:T(8,128)(2,1)S(1)} %pad_maximum_fusion), channel_id=1, source_target_pairs={{0,12},{12,0},{1,13},{13,1},{2,14},{14,2},{3,15},{15,3},{4,16},{16... | collective-permute-start | bytes 1769480 | tf_op jit(solution)/shard_map/ppermute | solution.py:126
  94.6 1.5 %collective-permute-done.9 = bf16[2,4,72,512]{3,2,1,0:T(8,128)(2,1)S(1)} collective-permute-done((bf16[2,4,72,512]{3,2,1,0:T(8,128)(2,1)S(1)}, bf16[2,4,72,512]{3,2,1,0:T(8,128)(2,1)S(1)}, u32[]{:S(2)}, u32[]{:S(2)}) %collective-permute-start.9) | collective-permute-done | bytes 589856 | tf_op jit(solution)/shard_map/ppermute | solution.py:126
  97.0 1.9 %collective-permute-start.10 = (bf16[128,512]{1,0:T(8,128)(2,1)S(1)}, bf16[128,512]{1,0:T(8,128)(2,1)S(1)}, u32[]{:S(2)}, u32[]{:S(2)}) collective-permute-start(bf16[128,512]{1,0:T(8,128)(2,1)S(1)} %fusion.6.vo_ref), channel_id=1, source_target_pairs={{0,24},{12,36},{24,48},{36,60},{48,72},{60,84},{72,96},{84,108},{9... | collective-permute-start | bytes 393224 | tf_op jit(solution)/shard_map/ppermute | solution.py:121
  98.9 2.0 %collective-permute-start.11 = (bf16[128,512]{1,0:T(8,128)(2,1)S(1)}, bf16[128,512]{1,0:T(8,128)(2,1)S(1)}, u32[]{:S(2)}, u32[]{:S(2)}) collective-permute-start(bf16[128,512]{1,0:T(8,128)(2,1)S(1)} %fusion.6.vo_ref), channel_id=1, source_target_pairs={{0,12},{12,24},{24,36},{36,48},{48,60},{60,72},{72,84},{84,96},{96... | collective-permute-start | bytes 393224 | tf_op jit(solution)/shard_map/ppermute | solution.py:121
  101.0 6.7 %probs.1 = (f32[4,384,1024]{2,1,0:T(8,128)}, bf16[128,512]{1,0:T(8,128)(2,1)S(1)}, bf16[128,512]{1,0:T(8,128)(2,1)S(1)}, f32[128,512]{1,0:T(8,128)S(1)}) custom-call(s32[1,128]{1,0:T(1,128)S(1)} %subtract_bitcast_fusion.start_ref, bf16[128,4096]{1,0:T(8,128)(2,1)} %bitcast.81, bf16[128,4096]{1,0:T(8,128)(2,1)} %bitcast.83, ...), custom_call_target="tpu_custom_call" | custom-call | flops 2000000000 | bytes 9000000 | tf_op jit(solution)/shard_map/probs/pallas_call | solution.py:88
  107.7 3.5 %collective-permute-start.14 = (bf16[128,512]{1,0:T(8,128)(2,1)S(1)}, bf16[128,512]{1,0:T(8,128)(2,1)S(1)}, u32[]{:S(2)}, u32[]{:S(2)}) collective-permute-start(bf16[128,512]{1,0:T(8,128)(2,1)S(1)} %get-tuple-element.14), channel_id=1, source_target_pairs={{12,0},{24,12},{36,24},{48,36},{60,48},{72,60},{84,72},{96,84},{10... | collective-permute-start | bytes 393224 | tf_op jit(solution)/shard_map/ppermute | solution.py:121
  111.2 3.9 %collective-permute-start.15 = (bf16[128,512]{1,0:T(8,128)(2,1)S(1)}, bf16[128,512]{1,0:T(8,128)(2,1)S(1)}, u32[]{:S(2)}, u32[]{:S(2)}) collective-permute-start(bf16[128,512]{1,0:T(8,128)(2,1)S(1)} %get-tuple-element.15), channel_id=1, source_target_pairs={{24,0},{36,12},{48,24},{60,36},{72,48},{84,60},{96,72},{108,84},{1... | collective-permute-start | bytes 393224 | tf_op jit(solution)/shard_map/ppermute | solution.py:121
  115.1 2.8 %copy-done.1 = f32[4,384,1024]{2,1,0:T(8,128)S(1)} copy-done((f32[4,384,1024]{2,1,0:T(8,128)S(1)}, f32[4,384,1024]{2,1,0:T(8,128)}, u32[]{:S(2)}) %copy-start.1) | copy-done | bytes 6291480
  117.9 4.9 %grads.1 = (bf16[128,512]{1,0:T(8,128)(2,1)S(1)}, bf16[128,512]{1,0:T(8,128)(2,1)S(1)}, f32[128,512]{1,0:T(8,128)S(1)}) custom-call(f32[4,384,1024]{2,1,0:T(8,128)S(1)} %copy-done.1, bf16[128,4096]{1,0:T(8,128)(2,1)} %bitcast.82, bf16[128,4096]{1,0:T(8,128)(2,1)} %bitcast.84, bf16[128,512]{1,0:T(8,128)(2,1)S(1)} %collective-permute-done.10.vf_ref, ...), custom_call_target="tpu_custom_call" | custom-call | flops 2000000000 | bytes 9000000 | tf_op jit(solution)/shard_map/grads/pallas_call | solution.py:104
  122.9 1.9 %collective-permute-start.12 = (bf16[128,512]{1,0:T(8,128)(2,1)S(1)}, bf16[128,512]{1,0:T(8,128)(2,1)S(1)}, u32[]{:S(2)}, u32[]{:S(2)}) collective-permute-start(bf16[128,512]{1,0:T(8,128)(2,1)S(1)} %get-tuple-element.11), channel_id=1, source_target_pairs={{12,0},{24,12},{36,24},{48,36},{60,48},{72,60},{84,72},{96,84},{10... | collective-permute-start | bytes 393224 | tf_op jit(solution)/shard_map/ppermute | solution.py:121
  124.8 2.4 %collective-permute-start.13 = (bf16[128,512]{1,0:T(8,128)(2,1)S(1)}, bf16[128,512]{1,0:T(8,128)(2,1)S(1)}, u32[]{:S(2)}, u32[]{:S(2)}) collective-permute-start(bf16[128,512]{1,0:T(8,128)(2,1)S(1)} %get-tuple-element.12), channel_id=1, source_target_pairs={{24,0},{36,12},{48,24},{60,36},{72,48},{84,60},{96,72},{108,84},{1... | collective-permute-start | bytes 393224 | tf_op jit(solution)/shard_map/ppermute | solution.py:121
  127.3 2.7 %fusion = bf16[1,128,4608]{2,1,0:T(8,128)(2,1)} fusion(bf16[4608,512]{1,0:T(8,128)(2,1)S(1)} %bitcast.75, bf16[128,512]{1,0:T(8,128)(2,1)S(1)} %collective-permute-done.15, f32[128,512]{1,0:T(8,128)S(1)} %get-tuple-element.13, bf16[128,512]{1,0:T(8,128)(2,1)S(1)} %collective-permute-done.14), kind=kOutput, calls=%fused_computation.1 | convolution fusion | flops 604897280 | bytes 6422528 | tf_op jit(solution)/shard_map/dot_general | solution.py:185
  129.9 4.8 %collective-permute-done.13 = bf16[128,512]{1,0:T(8,128)(2,1)S(1)} collective-permute-done((bf16[128,512]{1,0:T(8,128)(2,1)S(1)}, bf16[128,512]{1,0:T(8,128)(2,1)S(1)}, u32[]{:S(2)}, u32[]{:S(2)}) %collective-permute-start.13) | collective-permute-done | bytes 131104 | tf_op jit(solution)/shard_map/ppermute | solution.py:121
  (45 shorter events, 4.5 us)
Async XLA Ops:
  0.6 95.5 %copy-start = (bf16[1,128,4608]{2,1,0:T(8,128)(2,1)S(1)}, bf16[1,128,4608]{2,1,0:T(8,128)(2,1)}, u32[]{:S(2)}) copy-start(bf16[1,128,4608]{2,1,0:T(8,128)(2,1)} %param.6) | copy-start | bytes 3538948
  29.2 25.6 %all-to-all-start.1 = ((bf16[8,72,512]{2,1,0:T(8,128)(2,1)}), bf16[8,72,512]{2,1,0:T(8,128)(2,1)S(1)}, u32[]{:S(2)}, u32[]{:S(2)}) async-start(bf16[8,72,512]{2,1,0:T(8,128)(2,1)} %broadcast_in_dim.69), calls=%async_computation.1 | async-start | bytes 1179648 | tf_op jit(solution)/shard_map/all_to_all | solution.py:137
  36.3 64.6 %collective-permute-start = (bf16[128,512]{1,0:T(8,128)(2,1)}, bf16[128,512]{1,0:T(8,128)(2,1)S(1)}, u32[]{:S(2)}, u32[]{:S(2)}) collective-permute-start(bf16[128,512]{1,0:T(8,128)(2,1)} %bitcast.71), channel_id=1, source_target_pairs={{0,24},{12,36},{24,48},{36,60},{48,72},{60,84},{72,96},{84,108},{9... | collective-permute-start | bytes 393224 | tf_op jit(solution)/shard_map/ppermute | solution.py:121
  40.2 60.8 %collective-permute-start.1 = (bf16[128,512]{1,0:T(8,128)(2,1)}, bf16[128,512]{1,0:T(8,128)(2,1)S(1)}, u32[]{:S(2)}, u32[]{:S(2)}) collective-permute-start(bf16[128,512]{1,0:T(8,128)(2,1)} %bitcast.72), channel_id=1, source_target_pairs={{0,12},{12,24},{24,36},{36,48},{48,60},{60,72},{72,84},{84,96},{96... | collective-permute-start | bytes 393224 | tf_op jit(solution)/shard_map/ppermute | solution.py:121
  54.9 11.1 %collective-permute-start.2 = (bf16[4,72,512]{2,1,0:T(8,128)(2,1)S(1)}, bf16[4,72,512]{2,1,0:T(8,128)(2,1)S(1)}, u32[]{:S(2)}, u32[]{:S(2)}) collective-permute-start(bf16[4,72,512]{2,1,0:T(8,128)(2,1)S(1)} %get-tuple-element.20), channel_id=1, source_target_pairs={{0,24},{24,48},{48,72},{72,0},{1,25},{25,49},{49,73},{73,1},{2,26}... | collective-permute-start | bytes 884744 | tf_op jit(solution)/shard_map/ppermute | solution.py:126
  56.8 12.6 %collective-permute-start.4 = (bf16[4,72,512]{2,1,0:T(8,128)(2,1)S(1)}, bf16[4,72,512]{2,1,0:T(8,128)(2,1)S(1)}, u32[]{:S(2)}, u32[]{:S(2)}) collective-permute-start(bf16[4,72,512]{2,1,0:T(8,128)(2,1)S(1)} %get-tuple-element.20), channel_id=1, source_target_pairs={{0,72},{24,0},{48,24},{72,48},{1,73},{25,1},{49,25},{73,49},{2,74}... | collective-permute-start | bytes 884744 | tf_op jit(solution)/shard_map/ppermute | solution.py:126
  60.7 8.6 %collective-permute-start.3 = (bf16[4,72,512]{2,1,0:T(8,128)(2,1)S(1)}, bf16[4,72,512]{2,1,0:T(8,128)(2,1)S(1)}, u32[]{:S(2)}, u32[]{:S(2)}) collective-permute-start(bf16[4,72,512]{2,1,0:T(8,128)(2,1)S(1)} %get-tuple-element.19), channel_id=1, source_target_pairs={{0,24},{24,48},{48,72},{72,0},{1,25},{25,49},{49,73},{73,1},{2,26}... | collective-permute-start | bytes 884744 | tf_op jit(solution)/shard_map/ppermute | solution.py:126
  65.9 9.8 %collective-permute-start.5 = (bf16[4,72,512]{2,1,0:T(8,128)(2,1)S(1)}, bf16[4,72,512]{2,1,0:T(8,128)(2,1)S(1)}, u32[]{:S(2)}, u32[]{:S(2)}) collective-permute-start(bf16[4,72,512]{2,1,0:T(8,128)(2,1)S(1)} %get-tuple-element.19), channel_id=1, source_target_pairs={{0,72},{24,0},{48,24},{72,48},{1,73},{25,1},{49,25},{73,49},{2,74}... | collective-permute-start | bytes 884744 | tf_op jit(solution)/shard_map/ppermute | solution.py:126
  75.8 18.5 %collective-permute-start.8 = (bf16[6,4,72,512]{3,2,1,0:T(8,128)(2,1)S(1)}, bf16[6,4,72,512]{3,2,1,0:T(8,128)(2,1)S(1)}, u32[]{:S(2)}, u32[]{:S(2)}) collective-permute-start(bf16[6,4,72,512]{3,2,1,0:T(8,128)(2,1)S(1)} %bitcast_dynamic-update-slice_fusion.7), channel_id=1, source_target_pairs={{0,12},{12,0},{1,13},{13,1},{2,14},{14,2},{3,15},{15,3},{4,16},{16... | collective-permute-start | bytes 5308424 | tf_op jit(solution)/shard_map/ppermute | solution.py:126
  77.7 11.3 %collective-permute-start.6 = (bf16[4,72,512]{2,1,0:T(8,128)(2,1)S(1)}, bf16[4,72,512]{2,1,0:T(8,128)(2,1)S(1)}, u32[]{:S(2)}, u32[]{:S(2)}) collective-permute-start(bf16[4,72,512]{2,1,0:T(8,128)(2,1)S(1)} %collective-permute-done.2), channel_id=1, source_target_pairs={{0,24},{24,48},{48,72},{72,0},{1,25},{25,49},{49,73},{73,1},{2,26}... | collective-permute-start | bytes 884744 | tf_op jit(solution)/shard_map/ppermute | solution.py:126
  79.6 12.5 %collective-permute-start.7 = (bf16[4,72,512]{2,1,0:T(8,128)(2,1)S(1)}, bf16[4,72,512]{2,1,0:T(8,128)(2,1)S(1)}, u32[]{:S(2)}, u32[]{:S(2)}) collective-permute-start(bf16[4,72,512]{2,1,0:T(8,128)(2,1)S(1)} %collective-permute-done.5), channel_id=1, source_target_pairs={{0,72},{24,0},{48,24},{72,48},{1,73},{25,1},{49,25},{73,49},{2,74}... | collective-permute-start | bytes 884744 | tf_op jit(solution)/shard_map/ppermute | solution.py:126
  92.2 3.9 %collective-permute-start.9 = (bf16[2,4,72,512]{3,2,1,0:T(8,128)(2,1)S(1)}, bf16[2,4,72,512]{3,2,1,0:T(8,128)(2,1)S(1)}, u32[]{:S(2)}, u32[]{:S(2)}) collective-permute-start(bf16[2,4,72,512]{3,2,1,0:T(8,128)(2,1)S(1)} %pad_maximum_fusion), channel_id=1, source_target_pairs={{0,12},{12,0},{1,13},{13,1},{2,14},{14,2},{3,15},{15,3},{4,16},{16... | collective-permute-start | bytes 1769480 | tf_op jit(solution)/shard_map/ppermute | solution.py:126
  94.5 6.5 %copy-start.2 = (bf16[1,128,512]{2,1,0:T(8,128)(2,1)S(1)}, bf16[1,128,512]{2,1,0:T(8,128)(2,1)}, u32[]{:S(2)}) copy-start(bf16[1,128,512]{2,1,0:T(8,128)(2,1)} %param.9) | copy-start | bytes 393220
  97.0 18.1 %collective-permute-start.10 = (bf16[128,512]{1,0:T(8,128)(2,1)S(1)}, bf16[128,512]{1,0:T(8,128)(2,1)S(1)}, u32[]{:S(2)}, u32[]{:S(2)}) collective-permute-start(bf16[128,512]{1,0:T(8,128)(2,1)S(1)} %fusion.6.vo_ref), channel_id=1, source_target_pairs={{0,24},{12,36},{24,48},{36,60},{48,72},{60,84},{72,96},{84,108},{9... | collective-permute-start | bytes 393224 | tf_op jit(solution)/shard_map/ppermute | solution.py:121
  98.9 16.2 %collective-permute-start.11 = (bf16[128,512]{1,0:T(8,128)(2,1)S(1)}, bf16[128,512]{1,0:T(8,128)(2,1)S(1)}, u32[]{:S(2)}, u32[]{:S(2)}) collective-permute-start(bf16[128,512]{1,0:T(8,128)(2,1)S(1)} %fusion.6.vo_ref), channel_id=1, source_target_pairs={{0,12},{12,24},{24,36},{36,48},{48,60},{60,72},{72,84},{84,96},{96... | collective-permute-start | bytes 393224 | tf_op jit(solution)/shard_map/ppermute | solution.py:121
  107.7 19.6 %collective-permute-start.14 = (bf16[128,512]{1,0:T(8,128)(2,1)S(1)}, bf16[128,512]{1,0:T(8,128)(2,1)S(1)}, u32[]{:S(2)}, u32[]{:S(2)}) collective-permute-start(bf16[128,512]{1,0:T(8,128)(2,1)S(1)} %get-tuple-element.14), channel_id=1, source_target_pairs={{12,0},{24,12},{36,24},{48,36},{60,48},{72,60},{84,72},{96,84},{10... | collective-permute-start | bytes 393224 | tf_op jit(solution)/shard_map/ppermute | solution.py:121
  111.2 16.1 %collective-permute-start.15 = (bf16[128,512]{1,0:T(8,128)(2,1)S(1)}, bf16[128,512]{1,0:T(8,128)(2,1)S(1)}, u32[]{:S(2)}, u32[]{:S(2)}) collective-permute-start(bf16[128,512]{1,0:T(8,128)(2,1)S(1)} %get-tuple-element.15), channel_id=1, source_target_pairs={{24,0},{36,12},{48,24},{60,36},{72,48},{84,60},{96,72},{108,84},{1... | collective-permute-start | bytes 393224 | tf_op jit(solution)/shard_map/ppermute | solution.py:121
  115.1 2.8 %copy-start.1 = (f32[4,384,1024]{2,1,0:T(8,128)S(1)}, f32[4,384,1024]{2,1,0:T(8,128)}, u32[]{:S(2)}) copy-start(f32[4,384,1024]{2,1,0:T(8,128)} %get-tuple-element.9.p_ref) | copy-start | bytes 18874372
  122.9 7.1 %collective-permute-start.12 = (bf16[128,512]{1,0:T(8,128)(2,1)S(1)}, bf16[128,512]{1,0:T(8,128)(2,1)S(1)}, u32[]{:S(2)}, u32[]{:S(2)}) collective-permute-start(bf16[128,512]{1,0:T(8,128)(2,1)S(1)} %get-tuple-element.11), channel_id=1, source_target_pairs={{12,0},{24,12},{36,24},{48,36},{60,48},{72,60},{84,72},{96,84},{10... | collective-permute-start | bytes 393224 | tf_op jit(solution)/shard_map/ppermute | solution.py:121
  124.8 9.9 %collective-permute-start.13 = (bf16[128,512]{1,0:T(8,128)(2,1)S(1)}, bf16[128,512]{1,0:T(8,128)(2,1)S(1)}, u32[]{:S(2)}, u32[]{:S(2)}) collective-permute-start(bf16[128,512]{1,0:T(8,128)(2,1)S(1)} %get-tuple-element.12), channel_id=1, source_target_pairs={{24,0},{36,12},{48,24},{60,36},{72,48},{84,60},{96,72},{108,84},{1... | collective-permute-start | bytes 393224 | tf_op jit(solution)/shard_map/ppermute | solution.py:121

commit v2 on v1

--- a/solution.py
+++ b/solution.py
@@ -132,34 +132,35 @@
     return jnp.sum(taken, axis=1)
 
 
-def copies(block, axis):
-    count = lax.axis_size(axis)
-    return lax.all_to_all(jnp.broadcast_to(block[None], (count,) + block.shape), axis, 0, 0, tiled=True)
+def copies(block, axes, count, groups=None):
+    stacked_copies = jnp.broadcast_to(block[None], (count,) + block.shape)
+    return lax.all_to_all(stacked_copies, axes, 0, 0, axis_index_groups=groups, tiled=True)
 
 
 def gathered(weight):
     rows, width = weight.shape
     ny, nx, nc, nz = (lax.axis_size(a) for a in ("y", "x", "core", "z"))
-    me, core, low = lax.axis_index("x"), lax.axis_index("core"), lax.axis_size("y") // 2
-    mine = copies(weight, "z")
+    y, x, core = (lax.axis_index(a) for a in ("y", "x", "core"))
+    order = [*range(0, ny, 2), *range(1, ny, 2)]
+    groups = [[row * nx + (c + 2 * (row % 2)) % nx for row in order] for c in range(nx)]
+    mine = copies(weight, "z", nz)
     mine = mine.reshape(nz * rows, width)
-    mine = copies(mine, "y")
-    first, second = mine[:low], mine[low:]
-    left_a = ring(first, ("x",), 1)
-    right_b = ring(second, ("x",), -1)
-    left_b = ring(second, ("x",), 1)
-    right_a = ring(first, ("x",), -1)
-    far_a = ring(left_a, ("x",), 1)
-    far_b = ring(right_b, ("x",), -1)
-    early, late = (first, second, left_a, left_b, right_a, right_b), (far_a, far_b)
-    early_swapped = ring(jnp.stack(early), ("core",), 1).reshape((3,) + mine.shape)
-    late_swapped = ring(jnp.stack(late), ("core",), 1).reshape((1,) + mine.shape)
-    slots = [((me + i) & (nx - 1)) * nc for i in (0, nx - 1, 1, 2)]
-    whole = jnp.zeros((ny, nx * nc, nz * rows, width), weight.dtype)
-    for i, piece in enumerate(early + late):
-        whole = lax.dynamic_update_slice(whole, piece[:, None], (low * (i % 2), slots[i // 2] + core, 0, 0))
-    for i, piece in enumerate([early_swapped[j] for j in range(3)] + [late_swapped[0]]):
-        whole = lax.dynamic_update_slice(whole, piece[:, None], (0, slots[i] + 1 - core, 0, 0))
+    mine = copies(mine, ("y", "x"), ny, groups)
+    above = ring(mine, ("y",), 1)
+    left = ring(mine, ("x",), 1)
+    right = ring(mine, ("x",), -1)
+    blocks, offsets = (mine, above, left, right), (0, 2, nx - 1, 1)
+    swapped = ring(jnp.stack(blocks[:2]), ("core",), 1)
+    late = ring(jnp.stack(blocks[2:]), ("core",), 1)
+    whole = jnp.zeros((ny // 2, 2, nx * nc, nz * rows, width), weight.dtype)
+    pieces = [(b, o, core) for b, o in zip(blocks, offsets)]
+    pieces += [(b, o, 1 - core) for b, o in zip((swapped[0], swapped[1], late[0], late[1]), offsets)]
+    for block, offset, side in pieces:
+        color = x + 2 * (y % 2) + offset
+        for odd in range(2):
+            half = block[odd * ny // 2 : (odd + 1) * ny // 2, None, None]
+            slot = ((color + 2 * odd) & (nx - 1)) * nc + side
+            whole = lax.dynamic_update_slice(whole, half, (0, odd, slot, 0, 0))
     return whole.reshape(ny * nx * nc * nz * rows, width)
 
 
@@ -169,11 +170,13 @@
     starts = doc_starts(doc_lengths[0], first + jnp.arange(rows, dtype=jnp.int32)) - first
     whole_weight = gathered(value_weight)
     keys = key_states[0]
-    query, grad = (pltpu.with_memory_space_constraint(a[0], pltpu.HBM) for a in (queries, out_grad))
+    query, grad, own_keys = (
+        pltpu.with_memory_space_constraint(a[0], pltpu.HBM) for a in (queries, out_grad, key_states)
+    )
     keys_far = from_behind(keys, 2)
     keys_near = from_behind(keys, 1)
     probs, value_far, value_near, value_own = probs_call(
-        starts[None], query, grad, keys_far, keys_near, keys
+        starts[None], query, grad, keys_far, keys_near, own_keys
     )
     value_near = from_behind(value_near, -1)
     value_far = from_behind(value_far, -2)
@@ -181,7 +184,7 @@
     values = jnp.dot(features[0], whole_weight, preferred_element_type=jnp.float32).astype(jnp.bfloat16)
     far = from_behind(values, 2)
     near = from_behind(values, 1)
-    key_far, key_near, key_own = grads_call(probs, query, grad, far, near, values)
+    key_far, key_near, key_own = grads_call(probs, queries[0], out_grad[0], far, near, values)
     feature_grad = lax.dot_general(
         value_grad, whole_weight, (((1,), (1,)), ((), ())), preferred_element_type=jnp.float32
     ).astype(jnp.bfloat16)

time: 136 us -> 119 us (0.88)
  the two profiles are of different devices: /device:TPU:6 before, /device:TPU:31 now
where the time goes in v2:
time: 119 us; the launch traced here: 118 us
  starting transfers between devices  56.1 us (47%)
  blocking collectives  24.7 us (21%)
  waiting for transfers between devices  13.9 us (12%)
  Pallas kernels  10.7 us (9%)
  local copies, waits for them, and re-layouts  6.07 us (5%)
  matrix products  3.44 us (3%)
  other arithmetic  1.88 us (2%)
    ppermute x8, starting transfers between devices, from_behind(): return lax.ppermute(block, axes, route)  25.8 us
    all_to_all x1, blocking collectives, copies(): lax.all_to_all(stacked_copies, axes, 0, 0, axis_index_groups=groups, tile...  24.7 us
    ppermute x5, starting transfers between devices, ring(): lax.ppermute(block, axes, [(i, (i + distance) % count) for i in range(cou...  21.9 us
    ppermute x5, waiting for transfers between devices, ring(): lax.ppermute(block, axes, [(i, (i + distance) % count) for i in range(cou...  8.65 us
    all_to_all x1, starting transfers between devices, copies(): lax.all_to_all(stacked_copies, axes, 0, 0, axis_index_groups=groups, tile...  8.38 us
    pallas_call x1, Pallas kernels, probs_call(): pl.pallas_call(probs_kernel, grid=(KVHEADS,), in_specs=[pl.BlockSpec((1,...  6.65 us
    ppermute x8, waiting for transfers between devices, from_behind(): return lax.ppermute(block, axes, route)  4.9 us
    pallas_call x1, Pallas kernels, grads_call(): pl.pallas_call(grads_kernel, grid=(KVHEADS,), in_specs=[probs, wide, wide...  4.02 us
  transfers between devices with their start and end apart: 14, of which 6 were waited for; matrix products, arithmetic and copies ran while one was open for 5% of the time, Pallas kernels for 9%

profile of v2, /device:TPU:31, one launch (start us, length us, event | category | flops | bytes accessed | tf_op | source)
XLA Modules:
  0.0 117.9 jit_solution(3729720382830459383)
XLA Ops:
  0.6 0.8 broadcast_in_dim.91
  1.4 24.7 %all_to_all.10 = bf16[12,6,512]{2,1,0:T(8,128)(2,1)S(1)} all-to-all(bf16[12,6,512]{2,1,0:T(8,128)(2,1)S(1)} %broadcast_in_dim.91), channel_id=1, replica_groups=mesh['y'=8,'x'=4,'core'=2,'z'=12] {'z'}, dimensions={0} | all-to-all | bytes 147456 | tf_op jit(solution)/shard_map/all_to_all | solution.py:137
  26.2 0.9 broadcast_in_dim.93
  27.0 8.4 %all-to-all-start.1 = ((bf16[8,72,512]{2,1,0:T(8,128)(2,1)}), bf16[8,72,512]{2,1,0:T(8,128)(2,1)S(1)}, u32[]{:S(2)}, u32[]{:S(2)}) async-start(bf16[8,72,512]{2,1,0:T(8,128)(2,1)} %broadcast_in_dim.93), calls=%async_computation.1 | async-start | bytes 1179648 | tf_op jit(solution)/shard_map/all_to_all | solution.py:137
  35.4 4.3 %collective-permute-start = (bf16[128,512]{1,0:T(8,128)(2,1)}, bf16[128,512]{1,0:T(8,128)(2,1)S(1)}, u32[]{:S(2)}, u32[]{:S(2)}) collective-permute-start(bf16[128,512]{1,0:T(8,128)(2,1)} %bitcast.133), channel_id=1, source_target_pairs={{0,24},{12,36},{24,48},{36,60},{48,72},{60,84},{72,96},{84,108},{9... | collective-permute-start | bytes 393224 | tf_op jit(solution)/shard_map/ppermute | solution.py:121
  39.7 5.8 %collective-permute-start.1 = (bf16[128,512]{1,0:T(8,128)(2,1)}, bf16[128,512]{1,0:T(8,128)(2,1)S(1)}, u32[]{:S(2)}, u32[]{:S(2)}) collective-permute-start(bf16[128,512]{1,0:T(8,128)(2,1)} %bitcast.134), channel_id=1, source_target_pairs={{0,12},{12,24},{24,36},{36,48},{48,60},{60,72},{72,84},{84,96},{96... | collective-permute-start | bytes 393224 | tf_op jit(solution)/shard_map/ppermute | solution.py:121
  45.5 0.7 copy.42
  46.5 0.8 select_reduce_fusion
  47.3 0.4 all-to-all-done.1
  47.6 4.2 %collective-permute-start.2 = (bf16[8,72,512]{2,1,0:T(8,128)(2,1)S(1)}, bf16[8,72,512]{2,1,0:T(8,128)(2,1)S(1)}, u32[]{:S(2)}, u32[]{:S(2)}) collective-permute-start(bf16[8,72,512]{2,1,0:T(8,128)(2,1)S(1)} %all-to-all-done.1), channel_id=1, source_target_pairs={{0,96},{96,192},{192,288},{288,384},{384,480},{480,576},{576,672},... | collective-permute-start | bytes 1769480 | tf_op jit(solution)/shard_map/ppermute | solution.py:126
  51.9 4.1 %collective-permute-start.3 = (bf16[8,72,512]{2,1,0:T(8,128)(2,1)S(1)}, bf16[8,72,512]{2,1,0:T(8,128)(2,1)S(1)}, u32[]{:S(2)}, u32[]{:S(2)}) collective-permute-start(bf16[8,72,512]{2,1,0:T(8,128)(2,1)S(1)} %all-to-all-done.1), channel_id=1, source_target_pairs={{0,24},{24,48},{48,72},{72,0},{1,25},{25,49},{49,73},{73,1},{2,26}... | collective-permute-start | bytes 1769480 | tf_op jit(solution)/shard_map/ppermute | solution.py:126
  56.0 1.9 %collective-permute-start.4 = (bf16[8,72,512]{2,1,0:T(8,128)(2,1)S(1)}, bf16[8,72,512]{2,1,0:T(8,128)(2,1)S(1)}, u32[]{:S(2)}, u32[]{:S(2)}) collective-permute-start(bf16[8,72,512]{2,1,0:T(8,128)(2,1)S(1)} %all-to-all-done.1), channel_id=1, source_target_pairs={{0,72},{24,0},{48,24},{72,48},{1,73},{25,1},{49,25},{73,49},{2,74}... | collective-permute-start | bytes 1769480 | tf_op jit(solution)/shard_map/ppermute | solution.py:126
  57.9 0.4 broadcast_in_dim.90
  58.4 3.7 %collective-permute-done.2 = bf16[8,72,512]{2,1,0:T(8,128)(2,1)S(1)} collective-permute-done((bf16[8,72,512]{2,1,0:T(8,128)(2,1)S(1)}, bf16[8,72,512]{2,1,0:T(8,128)(2,1)S(1)}, u32[]{:S(2)}, u32[]{:S(2)}) %collective-permute-start.2) | collective-permute-done | bytes 589856 | tf_op jit(solution)/shard_map/ppermute | solution.py:126
  62.2 5.3 %collective-permute-start.5 = (bf16[2,8,72,512]{3,2,1,0:T(8,128)(2,1)S(1)}, bf16[2,8,72,512]{3,2,1,0:T(8,128)(2,1)S(1)}, u32[]{:S(2)}, u32[]{:S(2)}) collective-permute-start(bf16[2,8,72,512]{3,2,1,0:T(8,128)(2,1)S(1)} %pad_maximum_fusion), channel_id=1, source_target_pairs={{0,12},{12,0},{1,13},{13,1},{2,14},{14,2},{3,15},{15,3},{4,16},{16... | collective-permute-start | bytes 3538952 | tf_op jit(solution)/shard_map/ppermute | solution.py:126
  67.6 2.9 %collective-permute-done.4 = bf16[8,72,512]{2,1,0:T(8,128)(2,1)S(1)} collective-permute-done((bf16[8,72,512]{2,1,0:T(8,128)(2,1)S(1)}, bf16[8,72,512]{2,1,0:T(8,128)(2,1)S(1)}, u32[]{:S(2)}, u32[]{:S(2)}) %collective-permute-start.4) | collective-permute-done | bytes 589856 | tf_op jit(solution)/shard_map/ppermute | solution.py:126
  70.6 6.3 %collective-permute-start.6 = (bf16[2,8,72,512]{3,2,1,0:T(8,128)(2,1)S(1)}, bf16[2,8,72,512]{3,2,1,0:T(8,128)(2,1)S(1)}, u32[]{:S(2)}, u32[]{:S(2)}) collective-permute-start(bf16[2,8,72,512]{3,2,1,0:T(8,128)(2,1)S(1)} %pad_maximum_fusion.1), channel_id=1, source_target_pairs={{0,12},{12,0},{1,13},{13,1},{2,14},{14,2},{3,15},{15,3},{4,16},{16... | collective-permute-start | bytes 3538952 | tf_op jit(solution)/shard_map/ppermute | solution.py:126
  77.3 2.1 %collective-permute-done.6 = bf16[2,8,72,512]{3,2,1,0:T(8,128)(2,1)S(1)} collective-permute-done((bf16[2,8,72,512]{3,2,1,0:T(8,128)(2,1)S(1)}, bf16[2,8,72,512]{3,2,1,0:T(8,128)(2,1)S(1)}, u32[]{:S(2)}, u32[]{:S(2)}) %collective-permute-start.6) | collective-permute-done | bytes 1179680 | tf_op jit(solution)/shard_map/ppermute | solution.py:126
  79.5 0.8 fusion.6.vo_ref
  80.3 2.1 %collective-permute-start.7 = (bf16[128,512]{1,0:T(8,128)(2,1)S(1)}, bf16[128,512]{1,0:T(8,128)(2,1)S(1)}, u32[]{:S(2)}, u32[]{:S(2)}) collective-permute-start(bf16[128,512]{1,0:T(8,128)(2,1)S(1)} %fusion.6.vo_ref), channel_id=1, source_target_pairs={{0,24},{12,36},{24,48},{36,60},{48,72},{60,84},{72,96},{84,108},{9... | collective-permute-start | bytes 393224 | tf_op jit(solution)/shard_map/ppermute | solution.py:121
  82.4 3.4 %collective-permute-start.8 = (bf16[128,512]{1,0:T(8,128)(2,1)S(1)}, bf16[128,512]{1,0:T(8,128)(2,1)S(1)}, u32[]{:S(2)}, u32[]{:S(2)}) collective-permute-start(bf16[128,512]{1,0:T(8,128)(2,1)S(1)} %fusion.6.vo_ref), channel_id=1, source_target_pairs={{0,12},{12,24},{24,36},{36,48},{48,60},{60,72},{72,84},{84,96},{96... | collective-permute-start | bytes 393224 | tf_op jit(solution)/shard_map/ppermute | solution.py:121
  85.8 6.7 %probs.1 = (f32[4,384,1024]{2,1,0:T(8,128)}, bf16[128,512]{1,0:T(8,128)(2,1)S(1)}, bf16[128,512]{1,0:T(8,128)(2,1)S(1)}, f32[128,512]{1,0:T(8,128)S(1)}) custom-call(s32[1,128]{1,0:T(1,128)S(1)} %subtract_bitcast_fusion.start_ref, bf16[128,4096]{1,0:T(8,128)(2,1)} %bitcast.121, bf16[128,4096]{1,0:T(8,128)(2,1)} %bitcast.123, ...), custom_call_target="tpu_custom_call" | custom-call | flops 2000000000 | bytes 9000000 | tf_op jit(solution)/shard_map/probs/pallas_call | solution.py:88
  92.4 1.9 %collective-permute-start.11 = (bf16[128,512]{1,0:T(8,128)(2,1)S(1)}, bf16[128,512]{1,0:T(8,128)(2,1)S(1)}, u32[]{:S(2)}, u32[]{:S(2)}) collective-permute-start(bf16[128,512]{1,0:T(8,128)(2,1)S(1)} %get-tuple-element.14), channel_id=1, source_target_pairs={{12,0},{24,12},{36,24},{48,36},{60,48},{72,60},{84,72},{96,84},{10... | collective-permute-start | bytes 393224 | tf_op jit(solution)/shard_map/ppermute | solution.py:121
  94.4 2.5 %collective-permute-start.12 = (bf16[128,512]{1,0:T(8,128)(2,1)S(1)}, bf16[128,512]{1,0:T(8,128)(2,1)S(1)}, u32[]{:S(2)}, u32[]{:S(2)}) collective-permute-start(bf16[128,512]{1,0:T(8,128)(2,1)S(1)} %get-tuple-element.15), channel_id=1, source_target_pairs={{24,0},{36,12},{48,24},{60,36},{72,48},{84,60},{96,72},{108,84},{1... | collective-permute-start | bytes 393224 | tf_op jit(solution)/shard_map/ppermute | solution.py:121
  96.9 2.8 %copy-done.1 = f32[4,384,1024]{2,1,0:T(8,128)S(1)} copy-done((f32[4,384,1024]{2,1,0:T(8,128)S(1)}, f32[4,384,1024]{2,1,0:T(8,128)}, u32[]{:S(2)}) %copy-start.1) | copy-done | bytes 6291480
  99.7 4.0 %grads.1 = (bf16[128,512]{1,0:T(8,128)(2,1)S(1)}, bf16[128,512]{1,0:T(8,128)(2,1)S(1)}, f32[128,512]{1,0:T(8,128)S(1)}) custom-call(f32[4,384,1024]{2,1,0:T(8,128)S(1)} %copy-done.1, bf16[128,4096]{1,0:T(8,128)(2,1)S(1)} %bitcast.122, bf16[128,4096]{1,0:T(8,128)(2,1)S(1)} %bitcast.124, bf16[128,512]{1,0:T(8,128)(2,1)S(1)} %collective-permute-done.7.vf_ref, ...), custom_call_target="tpu_custom_call" | custom-call | flops 2000000000 | bytes 9000000 | tf_op jit(solution)/shard_map/grads/pallas_call | solution.py:104
  103.7 3.3 %collective-permute-start.10 = (bf16[128,512]{1,0:T(8,128)(2,1)S(1)}, bf16[128,512]{1,0:T(8,128)(2,1)S(1)}, u32[]{:S(2)}, u32[]{:S(2)}) collective-permute-start(bf16[128,512]{1,0:T(8,128)(2,1)S(1)} %get-tuple-element.12), channel_id=1, source_target_pairs={{24,0},{36,12},{48,24},{60,36},{72,48},{84,60},{96,72},{108,84},{1... | collective-permute-start | bytes 393224 | tf_op jit(solution)/shard_map/ppermute | solution.py:121
  107.0 2.6 %collective-permute-start.9 = (bf16[128,512]{1,0:T(8,128)(2,1)S(1)}, bf16[128,512]{1,0:T(8,128)(2,1)S(1)}, u32[]{:S(2)}, u32[]{:S(2)}) collective-permute-start(bf16[128,512]{1,0:T(8,128)(2,1)S(1)} %get-tuple-element.11), channel_id=1, source_target_pairs={{12,0},{24,12},{36,24},{48,36},{60,48},{72,60},{84,72},{96,84},{10... | collective-permute-start | bytes 393224 | tf_op jit(solution)/shard_map/ppermute | solution.py:121
  109.6 2.7 %fusion = bf16[1,128,4608]{2,1,0:T(8,128)(2,1)} fusion(bf16[4608,512]{1,0:T(8,128)(2,1)S(1)} %bitcast.126, bf16[128,512]{1,0:T(8,128)(2,1)S(1)} %collective-permute-done.12, f32[128,512]{1,0:T(8,128)S(1)} %get-tuple-element.13, bf16[128,512]{1,0:T(8,128)(2,1)S(1)} %collective-permute-done.11), kind=kOutput, calls=%fused_computation.1 | convolution fusion | flops 604897280 | bytes 6422528 | tf_op jit(solution)/shard_map/dot_general | solution.py:188
  112.3 0.5 collective-permute-done.10
  112.8 4.4 %collective-permute-done.9 = bf16[128,512]{1,0:T(8,128)(2,1)S(1)} collective-permute-done((bf16[128,512]{1,0:T(8,128)(2,1)S(1)}, bf16[128,512]{1,0:T(8,128)(2,1)S(1)}, u32[]{:S(2)}, u32[]{:S(2)}) %collective-permute-start.9) | collective-permute-done | bytes 131104 | tf_op jit(solution)/shard_map/ppermute | solution.py:121
  117.2 0.7 fusion.25
  (38 shorter events, 0.9 us)
Async XLA Ops:
  0.6 78.9 %copy-start = (bf16[1,128,4608]{2,1,0:T(8,128)(2,1)S(1)}, bf16[1,128,4608]{2,1,0:T(8,128)(2,1)}, u32[]{:S(2)}) copy-start(bf16[1,128,4608]{2,1,0:T(8,128)(2,1)} %param.6) | copy-start | bytes 3538948
  27.0 20.6 %all-to-all-start.1 = ((bf16[8,72,512]{2,1,0:T(8,128)(2,1)}), bf16[8,72,512]{2,1,0:T(8,128)(2,1)S(1)}, u32[]{:S(2)}, u32[]{:S(2)}) async-start(bf16[8,72,512]{2,1,0:T(8,128)(2,1)} %broadcast_in_dim.93), calls=%async_computation.1 | async-start | bytes 1179648 | tf_op jit(solution)/shard_map/all_to_all | solution.py:137
  35.4 50.4 %collective-permute-start = (bf16[128,512]{1,0:T(8,128)(2,1)}, bf16[128,512]{1,0:T(8,128)(2,1)S(1)}, u32[]{:S(2)}, u32[]{:S(2)}) collective-permute-start(bf16[128,512]{1,0:T(8,128)(2,1)} %bitcast.133), channel_id=1, source_target_pairs={{0,24},{12,36},{24,48},{36,60},{48,72},{60,84},{72,96},{84,108},{9... | collective-permute-start | bytes 393224 | tf_op jit(solution)/shard_map/ppermute | solution.py:121
  39.7 46.1 %collective-permute-start.1 = (bf16[128,512]{1,0:T(8,128)(2,1)}, bf16[128,512]{1,0:T(8,128)(2,1)S(1)}, u32[]{:S(2)}, u32[]{:S(2)}) collective-permute-start(bf16[128,512]{1,0:T(8,128)(2,1)} %bitcast.134), channel_id=1, source_target_pairs={{0,12},{12,24},{24,36},{36,48},{48,60},{60,72},{72,84},{84,96},{96... | collective-permute-start | bytes 393224 | tf_op jit(solution)/shard_map/ppermute | solution.py:121
  47.6 14.5 %collective-permute-start.2 = (bf16[8,72,512]{2,1,0:T(8,128)(2,1)S(1)}, bf16[8,72,512]{2,1,0:T(8,128)(2,1)S(1)}, u32[]{:S(2)}, u32[]{:S(2)}) collective-permute-start(bf16[8,72,512]{2,1,0:T(8,128)(2,1)S(1)} %all-to-all-done.1), channel_id=1, source_target_pairs={{0,96},{96,192},{192,288},{288,384},{384,480},{480,576},{576,672},... | collective-permute-start | bytes 1769480 | tf_op jit(solution)/shard_map/ppermute | solution.py:126
  51.9 15.7 %collective-permute-start.3 = (bf16[8,72,512]{2,1,0:T(8,128)(2,1)S(1)}, bf16[8,72,512]{2,1,0:T(8,128)(2,1)S(1)}, u32[]{:S(2)}, u32[]{:S(2)}) collective-permute-start(bf16[8,72,512]{2,1,0:T(8,128)(2,1)S(1)} %all-to-all-done.1), channel_id=1, source_target_pairs={{0,24},{24,48},{48,72},{72,0},{1,25},{25,49},{49,73},{73,1},{2,26}... | collective-permute-start | bytes 1769480 | tf_op jit(solution)/shard_map/ppermute | solution.py:126
  56.0 14.4 %collective-permute-start.4 = (bf16[8,72,512]{2,1,0:T(8,128)(2,1)S(1)}, bf16[8,72,512]{2,1,0:T(8,128)(2,1)S(1)}, u32[]{:S(2)}, u32[]{:S(2)}) collective-permute-start(bf16[8,72,512]{2,1,0:T(8,128)(2,1)S(1)} %all-to-all-done.1), channel_id=1, source_target_pairs={{0,72},{24,0},{48,24},{72,48},{1,73},{25,1},{49,25},{73,49},{2,74}... | collective-permute-start | bytes 1769480 | tf_op jit(solution)/shard_map/ppermute | solution.py:126
  62.2 14.9 %collective-permute-start.5 = (bf16[2,8,72,512]{3,2,1,0:T(8,128)(2,1)S(1)}, bf16[2,8,72,512]{3,2,1,0:T(8,128)(2,1)S(1)}, u32[]{:S(2)}, u32[]{:S(2)}) collective-permute-start(bf16[2,8,72,512]{3,2,1,0:T(8,128)(2,1)S(1)} %pad_maximum_fusion), channel_id=1, source_target_pairs={{0,12},{12,0},{1,13},{13,1},{2,14},{14,2},{3,15},{15,3},{4,16},{16... | collective-permute-start | bytes 3538952 | tf_op jit(solution)/shard_map/ppermute | solution.py:126
  70.6 8.8 %collective-permute-start.6 = (bf16[2,8,72,512]{3,2,1,0:T(8,128)(2,1)S(1)}, bf16[2,8,72,512]{3,2,1,0:T(8,128)(2,1)S(1)}, u32[]{:S(2)}, u32[]{:S(2)}) collective-permute-start(bf16[2,8,72,512]{3,2,1,0:T(8,128)(2,1)S(1)} %pad_maximum_fusion.1), channel_id=1, source_target_pairs={{0,12},{12,0},{1,13},{13,1},{2,14},{14,2},{3,15},{15,3},{4,16},{16... | collective-permute-start | bytes 3538952 | tf_op jit(solution)/shard_map/ppermute | solution.py:126
  80.3 16.6 %copy-start.2 = (bf16[1,128,4096]{2,1,0:T(8,128)(2,1)S(1)}, bf16[1,128,4096]{2,1,0:T(8,128)(2,1)}, u32[]{:S(2)}) copy-start(bf16[1,128,4096]{2,1,0:T(8,128)(2,1)} %param.8) | copy-start | bytes 3145732
  80.3 16.6 %copy-start.3 = (bf16[1,128,4096]{2,1,0:T(8,128)(2,1)S(1)}, bf16[1,128,4096]{2,1,0:T(8,128)(2,1)}, u32[]{:S(2)}) copy-start(bf16[1,128,4096]{2,1,0:T(8,128)(2,1)} %param.10) | copy-start | bytes 3145732
  80.3 16.6 %collective-permute-start.7 = (bf16[128,512]{1,0:T(8,128)(2,1)S(1)}, bf16[128,512]{1,0:T(8,128)(2,1)S(1)}, u32[]{:S(2)}, u32[]{:S(2)}) collective-permute-start(bf16[128,512]{1,0:T(8,128)(2,1)S(1)} %fusion.6.vo_ref), channel_id=1, source_target_pairs={{0,24},{12,36},{24,48},{36,60},{48,72},{60,84},{72,96},{84,108},{9... | collective-permute-start | bytes 393224 | tf_op jit(solution)/shard_map/ppermute | solution.py:121
  82.4 14.5 %collective-permute-start.8 = (bf16[128,512]{1,0:T(8,128)(2,1)S(1)}, bf16[128,512]{1,0:T(8,128)(2,1)S(1)}, u32[]{:S(2)}, u32[]{:S(2)}) collective-permute-start(bf16[128,512]{1,0:T(8,128)(2,1)S(1)} %fusion.6.vo_ref), channel_id=1, source_target_pairs={{0,12},{12,24},{24,36},{36,48},{48,60},{60,72},{72,84},{84,96},{96... | collective-permute-start | bytes 393224 | tf_op jit(solution)/shard_map/ppermute | solution.py:121
  92.4 17.2 %collective-permute-start.11 = (bf16[128,512]{1,0:T(8,128)(2,1)S(1)}, bf16[128,512]{1,0:T(8,128)(2,1)S(1)}, u32[]{:S(2)}, u32[]{:S(2)}) collective-permute-start(bf16[128,512]{1,0:T(8,128)(2,1)S(1)} %get-tuple-element.14), channel_id=1, source_target_pairs={{12,0},{24,12},{36,24},{48,36},{60,48},{72,60},{84,72},{96,84},{10... | collective-permute-start | bytes 393224 | tf_op jit(solution)/shard_map/ppermute | solution.py:121
  94.4 15.3 %collective-permute-start.12 = (bf16[128,512]{1,0:T(8,128)(2,1)S(1)}, bf16[128,512]{1,0:T(8,128)(2,1)S(1)}, u32[]{:S(2)}, u32[]{:S(2)}) collective-permute-start(bf16[128,512]{1,0:T(8,128)(2,1)S(1)} %get-tuple-element.15), channel_id=1, source_target_pairs={{24,0},{36,12},{48,24},{60,36},{72,48},{84,60},{96,72},{108,84},{1... | collective-permute-start | bytes 393224 | tf_op jit(solution)/shard_map/ppermute | solution.py:121
  96.9 2.8 %copy-start.1 = (f32[4,384,1024]{2,1,0:T(8,128)S(1)}, f32[4,384,1024]{2,1,0:T(8,128)}, u32[]{:S(2)}) copy-start(f32[4,384,1024]{2,1,0:T(8,128)} %get-tuple-element.9.p_ref) | copy-start | bytes 18874372
  103.7 9.0 %collective-permute-start.10 = (bf16[128,512]{1,0:T(8,128)(2,1)S(1)}, bf16[128,512]{1,0:T(8,128)(2,1)S(1)}, u32[]{:S(2)}, u32[]{:S(2)}) collective-permute-start(bf16[128,512]{1,0:T(8,128)(2,1)S(1)} %get-tuple-element.12), channel_id=1, source_target_pairs={{24,0},{36,12},{48,24},{60,36},{72,48},{84,60},{96,72},{108,84},{1... | collective-permute-start | bytes 393224 | tf_op jit(solution)/shard_map/ppermute | solution.py:121
  107.0 10.2 %collective-permute-start.9 = (bf16[128,512]{1,0:T(8,128)(2,1)S(1)}, bf16[128,512]{1,0:T(8,128)(2,1)S(1)}, u32[]{:S(2)}, u32[]{:S(2)}) collective-permute-start(bf16[128,512]{1,0:T(8,128)(2,1)S(1)} %get-tuple-element.11), channel_id=1, source_target_pairs={{12,0},{24,12},{36,24},{48,36},{60,48},{72,60},{84,72},{96,84},{10... | collective-permute-start | bytes 393224 | tf_op jit(solution)/shard_map/ppermute | solution.py:121
